TPU v7x, 32 devices: a whole 2x2x4 slice. The times are simulated.
32 devices in a mesh: sky: 4 (over y, x), vel: 8 (over z, core).
Axes of the slice: x: 2, y: 2, z: 4, core: 2. Of those that a mesh axis runs over, the one named last changes fastest.
Arguments:
- psi_maps: float32 [4, 2048, 512], P(None, ('sky', 'vel')), may hold values from -6 to 6
- phi_maps: float32 [4, 2048, 512], P(None, ('sky', 'vel')), may hold values from 0.25 to 4
- psf_taps: float32 [9], replicated, may hold values from 0.1 to 1
- shifts: int32 [64, 4, 2], P('vel'), may hold values from -16 to 16, as said below
Outputs:
- likelihood: float32 [64, 2048, 512], P('vel', 'sky')
Inputs may be any that keep to these rules, and one draw needn't show every extreme that they name: `shifts`: frame 0 has shift 0 in every trial.
All inputs are finite; a program needn't handle non-finite values.
Results may differ from a plain program's by a relative error of at most 0.0003.
Values sent between devices are 32-bit elements; how exact they have to be, the bound alone decides.
A program may use at most 128 MiB of HBM per device.

v0:
```python
import jax
import jax.numpy as jnp
from jax import lax
from jax.sharding import PartitionSpec as P

FRAMES = 4
SHIFT = 16


def padded(cells, sides, width):
    for axis, dim in sides:
        count = lax.axis_size(axis)
        ends = count - 1
        head = lax.slice_in_dim(cells, 0, width, axis=dim)
        tail = lax.slice_in_dim(cells, cells.shape[dim] - width, cells.shape[dim], axis=dim)
        cells = jnp.concatenate(
            [
                lax.ppermute(tail, axis, [(i, (i + 1) % count) for i in range(ends)]),
                cells,
                lax.ppermute(head, axis, [((i + 1) % count, i) for i in range(ends)]),
            ],
            axis=dim,
        )
    return cells


def band_matrix(weights, width):
    row_index = lax.broadcasted_iota(jnp.int32, (width, width), 0)
    col_index = lax.broadcasted_iota(jnp.int32, (width, width), 1)
    offsets = row_index - col_index + weights.shape[0] // 2
    matrix = jnp.zeros((width, width), weights.dtype)
    for position in range(weights.shape[0]):
        matrix = matrix + jnp.where(
            offsets == position, weights[position], jnp.zeros((), weights.dtype)
        )
    return matrix


def correlate(extended, weights, count):
    squared = weights * weights
    width = extended.shape[-1]
    along_psi = jnp.matmul(
        extended[0], band_matrix(weights, width), precision=lax.Precision.HIGHEST
    )
    along_phi = jnp.matmul(
        extended[1], band_matrix(squared, width), precision=lax.Precision.HIGHEST
    )
    blurred = jnp.stack([along_psi, along_phi])
    total = jnp.zeros(blurred.shape[:2] + (count, width), blurred.dtype)
    for position in range(weights.shape[0]):
        factor = jnp.stack([weights[position], squared[position]])
        total = total + factor[:, None, None, None] * blurred[:, :, position : position + count]
    return total


def per_device(psi_maps, phi_maps, psf_taps, shifts):
    weights = psf_taps / jnp.sum(psf_taps)
    half = psf_taps.shape[0] // 2
    stacked = jnp.stack([psi_maps, phi_maps])
    extended = padded(stacked, ((("sky", "vel"), 2),), half)
    share_blur = correlate(extended, weights, stacked.shape[2])
    blurred = lax.all_gather(share_blur, "vel", axis=2, tiled=True)
    row_count = blurred.shape[2]
    width = blurred.shape[3]
    reach = padded(blurred, (("sky", 2),), SHIFT)
    reach = jnp.pad(reach, ((0, 0), (0, 0), (0, 0), (SHIFT, SHIFT)))
    anchor = jnp.zeros((), jnp.int32)

    def stack_trial(shift_rows):
        total = jnp.zeros((2, row_count, width), reach.dtype)
        for frame in range(FRAMES):
            piece = lax.dynamic_slice(
                reach[:, frame],
                (anchor, SHIFT + shift_rows[frame, 0], SHIFT + shift_rows[frame, 1]),
                (2, row_count, width),
            )
            total = total + piece
        return total[0] / jnp.sqrt(total[1])

    return lax.map(stack_trial, shifts)


def solution(mesh):
    return jax.shard_map(
        per_device,
        mesh=mesh,
        in_specs=(
            P(None, ("sky", "vel"), None),
            P(None, ("sky", "vel"), None),
            P(),
            P("vel", None, None),
        ),
        out_specs=P("vel", "sky", None),
        check_vma=False,
    )
```

profile of v0, /device:TPU:3, one launch (start us, length us, event | category | flops | bytes accessed | tf_op | source)
XLA Modules:
  0.0 322.8 jit_solution(4517742748467950771)
XLA Ops:
  7.5 3.8 %collective-permute-start = (f32[2,4,4,512]{3,2,1,0:T(4,128)S(1)}, f32[2,4,4,512]{3,2,1,0:T(4,128)S(1)}, u32[]{:S(2)}, u32[]{:S(2)}) collective-permute-start(f32[2,4,4,512]{3,2,1,0:T(4,128)S(1)} %get-tuple-element.107), channel_id=1, source_target_pairs={{0,1},{1,2},{2,3},{3,4},{4,5},{5,6},{6,7},{7,8},{8,9},{9,10},{10,1... | collective-permute-start | bytes 196616 | tf_op jit(solution)/shard_map/ppermute | solution.py:18
  11.3 1.9 collective-permute-start.1
  20.3 1.4 pad_maximum_fusion.4
  21.8 1.4 pad_maximum_fusion.5
  23.1 1.4 pad_maximum_fusion.6
  28.5 1.4 pad_maximum_fusion
  29.9 7.0 %convolution_bitcast_fusion = f32[1,4,72,512]{3,2,1,0:T(8,128)S(1)} fusion(f32[2,4,72,512]{3,2,1,0:T(8,128)S(1)} %pad_maximum_fusion, f32[]{:T(128)} %bitcast.41, f32[]{:T(128)} %bitcast.40, f32[]{:T(128)} %bitcast.39, f32[]{:T(128)} %bitcast.38, f32[]{:T(128)} %bitcast.37, f32[]{:T(128)} %bitcast.36, f32[]{:T(128)} %bitcast.35, f32[]{:T(128)} %bitcast.34, ...), kind=kOutput, calls=%fused_computation.28 | convolution fusion | flops 913309696 | bytes 1179684 | tf_op jit(solution)/shard_map/dot_general | solution.py:45
  36.9 7.0 %convolution_bitcast_fusion.1 = f32[1,4,72,512]{3,2,1,0:T(8,128)S(1)} fusion(f32[2,4,72,512]{3,2,1,0:T(8,128)S(1)} %pad_maximum_fusion, f32[]{:T(128)} %bitcast.29, f32[]{:T(128)} %bitcast.28, f32[]{:T(128)} %bitcast.27, f32[]{:T(128)} %bitcast.26, f32[]{:T(128)} %bitcast.25, f32[]{:T(128)} %bitcast.24, f32[]{:T(128)} %bitcast.23, f32[]{:T(128)} %bitcast.22, ...), kind=kOutput, calls=%fused_computation.29 | convolution fusion | flops 913309696 | bytes 1179684 | tf_op jit(solution)/shard_map/dot_general | solution.py:42
  43.9 2.0 fusion.8
  46.0 83.7 %all-gather.2.cloned.1.call-done = f32[2,4,512,512]{3,2,1,0:T(8,128)} async-done(((f32[2,4,64,512]{3,2,1,0:T(8,128)}), f32[2,4,512,512]{3,2,1,0:T(8,128)}) %all-gather.2.cloned.1.call-update) | async-done | bytes 8388624 | tf_op jit(solution)/shard_map/all_gather | solution.py:62
  130.7 3.1 collective-permute-start.2
  133.8 2.2 collective-permute-start.3
  136.1 4.1 %collective-permute-done.2 = f32[2,4,16,512]{3,2,1,0:T(8,128)S(1)} collective-permute-done((f32[2,4,16,512]{3,2,1,0:T(8,128)S(1)}, f32[2,4,16,512]{3,2,1,0:T(8,128)S(1)}, u32[]{:S(2)}, u32[]{:S(2)}) %collective-permute-start.2) | collective-permute-done | bytes 262176 | tf_op jit(solution)/shard_map/ppermute | solution.py:18
  140.2 6.5 %collective-permute-done.3 = f32[2,4,16,512]{3,2,1,0:T(8,128)S(1)} collective-permute-done((f32[2,4,16,512]{3,2,1,0:T(8,128)S(1)}, f32[2,4,16,512]{3,2,1,0:T(8,128)S(1)}, u32[]{:S(2)}, u32[]{:S(2)}) %collective-permute-start.3) | collective-permute-done | bytes 262176 | tf_op jit(solution)/shard_map/ppermute | solution.py:20
  146.7 11.0 %select_maximum_fusion = f32[2,4,544,544]{3,2,1,0:T(8,128)} fusion(f32[2,4,16,512]{3,2,1,0:T(8,128)S(1)} %collective-permute-done.3, f32[2,4,512,512]{3,2,1,0:T(8,128)} %all-gather.2.cloned.1.call-done, f32[2,4,16,512]{3,2,1,0:T(8,128)S(1)} %collective-permute-done.2), kind=kLoop, calls=%fused_computation.9 | loop fusion | flops 18939904 | bytes 18382848 | tf_op jit(solution)/shard_map/concatenate | solution.py:16
  157.8 158.2 %while.13 = (s32[]{:T(128)}, f32[8,512,512]{2,1,0:T(8,128)}, f32[2,4,544,544]{3,2,1,0:T(8,128)}, s32[8,4,2]{1,2,0:T(2,128)S(1)}, s32[]{:T(128)}, /*index=5*/s32[1,1]{0,1:T(1,128)}, s32[]{:T(128)}, s32[1,1]{0,1:T(1,128)}) while((s32[]{:T(128)}, f32[8,512,512]{2,1,0:T(8,128)}, f32[2,4,544,544]{3,2,1,0:T(8,128)}, s32[8,4,2]{1,2,0:T(2,128)S(1)}, ...), condition=%wide.region_2.3_spmd, body=%wide.region_1.2_spmd.sunk | while | flops 1835042 | bytes 32572504 | solution.py:80
  168.9 5.1 %fusion.161 = (f32[2,1,544,544]{3,2,1,0:T(8,128)S(1)}, f32[2,1,544,544]{3,2,1,0:T(8,128)S(1)}, f32[2,1,544,544]{3,2,1,0:T(8,128)S(1)}, f32[2,1,544,544]{3,2,1,0:T(8,128)S(1)}) fusion(f32[2,4,544,544]{3,2,1,0:T(8,128)} %get-tuple-element.203), kind=kLoop, calls=%fused_computation.176.clone.1 | loop fusion | bytes 18939904 | tf_op jit(solution)/shard_map/while/body/eval_jaxpr/slice | solution.py:73
  174.0 2.4 dynamic-slice_add_fusion.2
  188.7 5.1 %fusion.161 = (f32[2,1,544,544]{3,2,1,0:T(8,128)S(1)}, f32[2,1,544,544]{3,2,1,0:T(8,128)S(1)}, f32[2,1,544,544]{3,2,1,0:T(8,128)S(1)}, f32[2,1,544,544]{3,2,1,0:T(8,128)S(1)}) fusion(f32[2,4,544,544]{3,2,1,0:T(8,128)} %get-tuple-element.203), kind=kLoop, calls=%fused_computation.176.clone.1 | loop fusion | bytes 18939904 | tf_op jit(solution)/shard_map/while/body/eval_jaxpr/slice | solution.py:73
  193.8 2.3 dynamic-slice_add_fusion.2
  208.5 5.1 %fusion.161 = (f32[2,1,544,544]{3,2,1,0:T(8,128)S(1)}, f32[2,1,544,544]{3,2,1,0:T(8,128)S(1)}, f32[2,1,544,544]{3,2,1,0:T(8,128)S(1)}, f32[2,1,544,544]{3,2,1,0:T(8,128)S(1)}) fusion(f32[2,4,544,544]{3,2,1,0:T(8,128)} %get-tuple-element.203), kind=kLoop, calls=%fused_computation.176.clone.1 | loop fusion | bytes 18939904 | tf_op jit(solution)/shard_map/while/body/eval_jaxpr/slice | solution.py:73
  213.6 2.3 dynamic-slice_add_fusion.2
  228.2 5.1 %fusion.161 = (f32[2,1,544,544]{3,2,1,0:T(8,128)S(1)}, f32[2,1,544,544]{3,2,1,0:T(8,128)S(1)}, f32[2,1,544,544]{3,2,1,0:T(8,128)S(1)}, f32[2,1,544,544]{3,2,1,0:T(8,128)S(1)}) fusion(f32[2,4,544,544]{3,2,1,0:T(8,128)} %get-tuple-element.203), kind=kLoop, calls=%fused_computation.176.clone.1 | loop fusion | bytes 18939904 | tf_op jit(solution)/shard_map/while/body/eval_jaxpr/slice | solution.py:73
  233.3 2.3 dynamic-slice_add_fusion.2
  248.0 5.1 %fusion.161 = (f32[2,1,544,544]{3,2,1,0:T(8,128)S(1)}, f32[2,1,544,544]{3,2,1,0:T(8,128)S(1)}, f32[2,1,544,544]{3,2,1,0:T(8,128)S(1)}, f32[2,1,544,544]{3,2,1,0:T(8,128)S(1)}) fusion(f32[2,4,544,544]{3,2,1,0:T(8,128)} %get-tuple-element.203), kind=kLoop, calls=%fused_computation.176.clone.1 | loop fusion | bytes 18939904 | tf_op jit(solution)/shard_map/while/body/eval_jaxpr/slice | solution.py:73
  253.1 2.4 dynamic-slice_add_fusion.2
  267.8 5.1 %fusion.161 = (f32[2,1,544,544]{3,2,1,0:T(8,128)S(1)}, f32[2,1,544,544]{3,2,1,0:T(8,128)S(1)}, f32[2,1,544,544]{3,2,1,0:T(8,128)S(1)}, f32[2,1,544,544]{3,2,1,0:T(8,128)S(1)}) fusion(f32[2,4,544,544]{3,2,1,0:T(8,128)} %get-tuple-element.203), kind=kLoop, calls=%fused_computation.176.clone.1 | loop fusion | bytes 18939904 | tf_op jit(solution)/shard_map/while/body/eval_jaxpr/slice | solution.py:73
  272.9 2.3 dynamic-slice_add_fusion.2
  287.6 5.1 %fusion.161 = (f32[2,1,544,544]{3,2,1,0:T(8,128)S(1)}, f32[2,1,544,544]{3,2,1,0:T(8,128)S(1)}, f32[2,1,544,544]{3,2,1,0:T(8,128)S(1)}, f32[2,1,544,544]{3,2,1,0:T(8,128)S(1)}) fusion(f32[2,4,544,544]{3,2,1,0:T(8,128)} %get-tuple-element.203), kind=kLoop, calls=%fused_computation.176.clone.1 | loop fusion | bytes 18939904 | tf_op jit(solution)/shard_map/while/body/eval_jaxpr/slice | solution.py:73
  292.6 2.3 dynamic-slice_add_fusion.2
  307.3 5.1 %fusion.161 = (f32[2,1,544,544]{3,2,1,0:T(8,128)S(1)}, f32[2,1,544,544]{3,2,1,0:T(8,128)S(1)}, f32[2,1,544,544]{3,2,1,0:T(8,128)S(1)}, f32[2,1,544,544]{3,2,1,0:T(8,128)S(1)}) fusion(f32[2,4,544,544]{3,2,1,0:T(8,128)} %get-tuple-element.203), kind=kLoop, calls=%fused_computation.176.clone.1 | loop fusion | bytes 18939904 | tf_op jit(solution)/shard_map/while/body/eval_jaxpr/slice | solution.py:73
  312.4 2.3 dynamic-slice_add_fusion.2
  (43 shorter events, 28.3 us)
Async XLA Ops:
  6.5 123.1 %all-gather.2.cloned.1.call-start = ((), (), s32[]{:S(2)}) async-start(), calls=%async_computation | async-start | bytes 9437184 | tf_op jit(solution)/shard_map/all_gather | solution.py:62
  7.5 21.0 %collective-permute-start = (f32[2,4,4,512]{3,2,1,0:T(4,128)S(1)}, f32[2,4,4,512]{3,2,1,0:T(4,128)S(1)}, u32[]{:S(2)}, u32[]{:S(2)}) collective-permute-start(f32[2,4,4,512]{3,2,1,0:T(4,128)S(1)} %get-tuple-element.107), channel_id=1, source_target_pairs={{0,1},{1,2},{2,3},{3,4},{4,5},{5,6},{6,7},{7,8},{8,9},{9,10},{10,1... | collective-permute-start | bytes 196616 | tf_op jit(solution)/shard_map/ppermute | solution.py:18
  11.3 17.2 %collective-permute-start.1 = (f32[2,4,4,512]{3,2,1,0:T(4,128)S(1)}, f32[2,4,4,512]{3,2,1,0:T(4,128)S(1)}, u32[]{:S(2)}, u32[]{:S(2)}) collective-permute-start(f32[2,4,4,512]{3,2,1,0:T(4,128)S(1)} %get-tuple-element.108), channel_id=1, source_target_pairs={{1,0},{2,1},{3,2},{4,3},{5,4},{6,5},{7,6},{8,7},{9,8},{10,9},{11,1... | collective-permute-start | bytes 196616 | tf_op jit(solution)/shard_map/ppermute | solution.py:20
  43.9 92.2 %copy-start = (s32[8,4,2]{0,2,1:T(2,128)S(1)}, s32[8,4,2]{0,2,1:T(2,128)}, u32[]{:S(2)}) copy-start(s32[8,4,2]{0,2,1:T(2,128)} %param.9) | copy-start | bytes 772
  130.7 9.5 %collective-permute-start.2 = (f32[2,4,16,512]{3,2,1,0:T(8,128)S(1)}, f32[2,4,16,512]{3,2,1,0:T(8,128)S(1)}, u32[]{:S(2)}, u32[]{:S(2)}) collective-permute-start(f32[2,4,16,512]{3,2,1,0:T(8,128)S(1)} %get-tuple-element.105), channel_id=1, source_target_pairs={{0,8},{8,16},{16,24},{1,9},{9,17},{17,25},{2,10},{10,18},{18,26},{... | collective-permute-start | bytes 786440 | tf_op jit(solution)/shard_map/ppermute | solution.py:18
  133.8 12.9 %collective-permute-start.3 = (f32[2,4,16,512]{3,2,1,0:T(8,128)S(1)}, f32[2,4,16,512]{3,2,1,0:T(8,128)S(1)}, u32[]{:S(2)}, u32[]{:S(2)}) collective-permute-start(f32[2,4,16,512]{3,2,1,0:T(8,128)S(1)} %get-tuple-element.106), channel_id=1, source_target_pairs={{8,0},{16,8},{24,16},{9,1},{17,9},{25,17},{10,2},{18,10},{26,18},{... | collective-permute-start | bytes 786440 | tf_op jit(solution)/shard_map/ppermute | solution.py:20
Sparse Core Ops, SparseCore 0:
  46.1 83.5 all-gather.1
where the time goes:
time: 327 us; the launch traced here: 323 us
  waiting for transfers between devices  94.3 us (29%)
  loops' own time  84 us (26%)
  other arithmetic  58.2 us (18%)
  local copies, waits for them, and re-layouts  47.8 us (15%)
  matrix products  14 us (4%)
  between operations  13.5 us (4%)
  starting transfers between devices  11 us (3%)
    another operation x1, loops' own time, per_device(): return lax.map(stack_trial, shifts)  84 us
    all_gather x1, waiting for transfers between devices, per_device(): blurred = lax.all_gather(share_blur, 'vel', axis=2, tiled=True)  83.7 us
    slice x8, local copies, waits for them, and re-layouts, stack_trial(): reach[:, frame]  40.5 us
    add x8, other arithmetic, stack_trial(): total = total + piece  18.6 us
    concatenate x2, other arithmetic, padded(): jnp.concatenate([lax.ppermute(tail, axis, [(i, (i + 1) % count) for i in...  12.4 us
    another operation x9, other arithmetic, correlate(): factor = jnp.stack([weights[position], squared[position]])  12 us
    dynamic_update_slice x8, other arithmetic, per_device(): return lax.map(stack_trial, shifts)  9.58 us
    dot_general x1, matrix products, correlate(): jnp.matmul(extended[0], band_matrix(weights, width), precision=lax.Precis...  7 us
  transfers between devices with their start and end apart: 5, of which 3 were waited for; matrix products, arithmetic and copies ran while one was open for 5% of the time, Pallas kernels for 0%

commit v1 on v0

v1 whole, which is shorter than its diff:
```python
import functools
import jax
import jax.numpy as jnp
from jax import lax
from jax.experimental import pallas as pl
from jax.experimental.pallas import tpu as pltpu
from jax.sharding import PartitionSpec as P

SHIFT = 16
EDGE = 24
LANES = 128
MESH = pl.DeviceIdType.MESH


def gather_kernel(
    vels, skies, taps_ref, psi_ref, phi_ref, out_ref,
    raw, along, top, bottom, band, weight,
    own_sem, recv_sem, right_sem, left_sem, pair_sem, top_recv, bottom_recv, top_send, bottom_send,
):
    frames, share, width = psi_ref.shape
    taps = taps_ref.shape[0]
    half = taps // 2
    maps = 2 * frames
    chips = vels // 2
    tiles = width // LANES
    both = 2 * share
    rows = vels * share
    sky = lax.axis_index("sky")
    vel = lax.axis_index("vel")
    chip = vel // 2
    core = vel % 2
    has_right = chip < chips - 1
    has_left = chip > 0
    has_next = sky < skies - 1
    has_prev = sky > 0

    own_psi = pltpu.make_async_copy(psi_ref, raw.at[vel, pl.ds(0, frames)], own_sem.at[0])
    own_phi = pltpu.make_async_copy(phi_ref, raw.at[vel, pl.ds(frames, frames)], own_sem.at[1])
    own_psi.start()
    own_phi.start()

    neighbours = (
        (has_right, (sky, vel + 2)),
        (has_left, (sky, vel - 2)),
        (has_next, (sky + 1, vel)),
        (has_prev, (sky - 1, vel)),
    )
    partner = (sky, vel + 1 - 2 * core)
    barrier = pltpu.get_barrier_semaphore()
    pl.semaphore_signal(barrier, inc=1, device_id=partner, device_id_type=MESH)
    for present, device in neighbours:

        @pl.when(present)
        def _(device=device):
            pl.semaphore_signal(barrier, inc=1, device_id=device, device_id_type=MESH)

    peers = 1
    for present, _ in neighbours:
        peers = peers + present.astype(jnp.int32)
    pl.semaphore_wait(barrier, peers)
    own_psi.wait()
    own_phi.wait()

    def line_copy(origin, m, to_right):
        chunk = 2 * origin + core
        return pltpu.make_async_remote_copy(
            src_ref=raw.at[chunk, m],
            dst_ref=raw.at[chunk, m],
            send_sem=(right_sem if to_right else left_sem).at[origin, m],
            recv_sem=recv_sem.at[chunk, m],
            device_id=(sky, vel + 2) if to_right else (sky, vel - 2),
            device_id_type=MESH,
        )

    def pair_copy(origin, m, side):
        chunk = 2 * origin + side
        return pltpu.make_async_remote_copy(
            src_ref=raw.at[chunk, m],
            dst_ref=raw.at[chunk, m],
            send_sem=pair_sem.at[origin, m],
            recv_sem=recv_sem.at[chunk, m],
            device_id=partner,
            device_id_type=MESH,
        )

    def top_copy(m):
        return pltpu.make_async_remote_copy(
            src_ref=raw.at[vels - 1, m, pl.ds(share - EDGE, EDGE)],
            dst_ref=top.at[m],
            send_sem=top_send.at[m],
            recv_sem=top_recv.at[m],
            device_id=(sky + 1, vel),
            device_id_type=MESH,
        )

    def bottom_copy(m):
        return pltpu.make_async_remote_copy(
            src_ref=raw.at[0, m, pl.ds(0, EDGE)],
            dst_ref=bottom.at[m],
            send_sem=bottom_send.at[m],
            recv_sem=bottom_recv.at[m],
            device_id=(sky - 1, vel),
            device_id_type=MESH,
        )

    def send_own(m, carry):
        @pl.when(has_right)
        def _():
            line_copy(chip, m, True).start()

        @pl.when(has_left)
        def _():
            line_copy(chip, m, False).start()

        pair_copy(chip, m, core).start()
        return carry

    lax.fori_loop(0, maps, send_own, 0)

    total = taps_ref[0]
    for i in range(1, taps):
        total = total + taps_ref[i]
    scale = 1.0 / jnp.full((8, LANES), total, jnp.float32)
    for i in range(taps):
        value = jnp.full((8, LANES), taps_ref[i], jnp.float32) * scale
        weight[0, i] = value
        weight[1, i] = value * value
    place = lax.broadcasted_iota(jnp.int32, (2 * LANES, LANES), 0)
    place = place - lax.broadcasted_iota(jnp.int32, (2 * LANES, LANES), 1)
    place = place - (LANES - SHIFT - half)
    for kind in range(2):
        matrix = jnp.zeros((2 * LANES, LANES), jnp.float32)
        for i in range(taps):
            value = jnp.broadcast_to(weight[kind, i][:1], (2 * LANES, LANES))
            matrix = jnp.where(place == i, value, matrix)
        coarse = matrix.astype(jnp.bfloat16)
        band[kind, 0] = coarse
        band[kind, 1] = (matrix - coarse.astype(jnp.float32)).astype(jnp.bfloat16)

    def blur_along(block, m, start):
        kind = m // frames
        count = block.shape[0]
        coarse = block.astype(jnp.bfloat16)
        fine = (block - coarse.astype(jnp.float32)).astype(jnp.bfloat16)
        for tile in range(tiles + 1):
            first, last = max(tile - 1, 0), min(tile + 1, tiles)
            columns = slice(first * LANES, last * LANES)
            offset = (first - tile + 1) * LANES
            depth = (last - first) * LANES
            high = band[kind, 0, offset : offset + depth]
            low = band[kind, 1, offset : offset + depth]
            value = jnp.dot(coarse[:, columns], high, preferred_element_type=jnp.float32)
            value += jnp.dot(fine[:, columns], high, preferred_element_type=jnp.float32)
            value += jnp.dot(coarse[:, columns], low, preferred_element_type=jnp.float32)
            if tile in (0, tiles):
                lane = lax.broadcasted_iota(jnp.int32, (count, LANES), 1)
                value = jnp.where(lane >= SHIFT if tile == 0 else lane < SHIFT, value, 0.0)
            along[m, tile, pl.ds(start, count)] = value

    def blur_across(m, start, count):
        kind = m // frames
        factors = [weight[kind, i] for i in range(taps)]

        def one_tile(tile, carry):
            for group in range(count // 8):
                base = start + 8 * group
                value = factors[0] * along[m, tile, pl.ds(base + 8 - half, 8)]
                for i in range(1, taps):
                    value += factors[i] * along[m, tile, pl.ds(base + 8 - half + i, 8)]
                out_ref[m, tile, pl.ds(pl.multiple_of(base, 8), 8)] = value
            return carry

        lax.fori_loop(0, tiles + 1, one_tile, 0)

    def arrive(distance, m):
        left = chip - distance
        right = chip + distance

        @pl.when((distance > 0) & (left >= 0))
        def _():
            line_copy(left, m, True).wait_recv()

            @pl.when(has_right)
            def _():
                line_copy(left, m, True).start()

            pair_copy(left, m, core).start()

        @pl.when((distance > 0) & (right < chips))
        def _():
            line_copy(right, m, False).wait_recv()

            @pl.when(has_left)
            def _():
                line_copy(right, m, False).start()

            pair_copy(right, m, core).start()

    def process(distance, m):
        def one_side(side, carry):
            origin = chip + (2 * side - 1) * distance

            @pl.when((origin >= 0) & (origin < chips) & ((side == 0) | (distance > 0)))
            def _():
                pair_copy(origin, m, 1 - core).wait_recv()

                @pl.when((origin == chips - 1) & has_next)
                def _():
                    top_copy(m).start()

                @pl.when((origin == 0) & has_prev)
                def _():
                    bottom_copy(m).start()

                def one_chunk(chunk, carry):
                    start = pl.multiple_of(EDGE + chunk * share, 8)
                    blur_along(raw[chunk, m], m, start)
                    return carry

                lax.fori_loop(2 * origin, 2 * origin + 2, one_chunk, 0)

                @pl.when(distance == 0)
                def _():
                    blur_across(m, SHIFT + origin * both + 8, both - 16)

                @pl.when(distance > 0)
                def _():
                    blur_across(m, SHIFT + origin * both + 8 - 16 * side, both)

            return carry

        lax.fori_loop(0, 2, one_side, 0)

    def step(index, carry):
        @pl.when(index < chips * maps)
        def _():
            arrive(index // maps, index % maps)

        @pl.when(index > 0)
        def _():
            process((index - 1) // maps, (index - 1) % maps)

        return carry

    lax.fori_loop(0, chips * maps + 1, step, 0)

    def finish(m, carry):
        @pl.when(has_prev)
        def _():
            pltpu.make_async_copy(top.at[m], top.at[m], top_recv.at[m]).wait()
            blur_along(top[m], m, 0)
            blur_across(m, 0, EDGE)

        @pl.when(jnp.logical_not(has_prev))
        def _():
            for tile in range(tiles + 1):
                along[m, tile, pl.ds(0, EDGE)] = jnp.zeros((EDGE, LANES), jnp.float32)
            blur_across(m, SHIFT, 8)
            for tile in range(tiles + 1):
                out_ref[m, tile, pl.ds(0, SHIFT)] = jnp.zeros((SHIFT, LANES), jnp.float32)

        @pl.when(has_next)
        def _():
            pltpu.make_async_copy(bottom.at[m], bottom.at[m], bottom_recv.at[m]).wait()
            blur_along(bottom[m], m, EDGE + rows)
            blur_across(m, SHIFT + rows - 8, EDGE)

        @pl.when(jnp.logical_not(has_next))
        def _():
            for tile in range(tiles + 1):
                along[m, tile, pl.ds(EDGE + rows, EDGE)] = jnp.zeros((EDGE, LANES), jnp.float32)
            blur_across(m, SHIFT + rows - 8, 8)
            for tile in range(tiles + 1):
                out_ref[m, tile, pl.ds(SHIFT + rows, SHIFT)] = jnp.zeros((SHIFT, LANES), jnp.float32)

        return carry

    lax.fori_loop(0, maps, finish, 0)

    def drain(index, carry):
        origin = index // maps
        m = index % maps

        @pl.when(has_right & (origin <= chip))
        def _():
            line_copy(origin, m, True).wait_send()

        @pl.when(has_left & (origin >= chip))
        def _():
            line_copy(origin, m, False).wait_send()

        pair_copy(origin, m, core).wait_send()

        @pl.when((origin == 0) & has_next)
        def _():
            top_copy(m).wait_send()

        @pl.when((origin == 0) & has_prev)
        def _():
            bottom_copy(m).wait_send()

        return carry

    lax.fori_loop(0, chips * maps, drain, 0)


def stack_kernel(shifts_ref, maps_ref, out_ref):
    frames = shifts_ref.shape[1]
    tiles = maps_ref.shape[1]
    trial = pl.program_id(0)
    lane = lax.broadcasted_iota(jnp.int32, (8, LANES), 1)
    down, turn, inside = [], [], []
    for frame in range(frames):
        offset = shifts_ref[trial, frame, 1] + SHIFT
        down.append(shifts_ref[trial, frame, 0] + SHIFT)
        turn.append(lax.rem(LANES - offset, LANES))
        inside.append(lane < LANES - offset)

    def one_group(group, carry):
        base = group * 8

        def stacked(kind):
            total = [None] * (tiles - 1)
            for frame in range(frames):
                m = kind * frames + frame
                rolled = [
                    pltpu.roll(maps_ref[m, tile, pl.ds(base + down[frame], 8)], turn[frame], 1)
                    for tile in range(tiles)
                ]
                for tile in range(tiles - 1):
                    piece = jnp.where(inside[frame], rolled[tile], rolled[tile + 1])
                    total[tile] = piece if frame == 0 else total[tile] + piece
            return total

        psi = stacked(0)
        phi = stacked(1)
        for tile in range(tiles - 1):
            out_ref[0, pl.ds(pl.multiple_of(base, 8), 8), tile * LANES : (tile + 1) * LANES] = (
                psi[tile] * lax.rsqrt(phi[tile])
            )
        return carry

    lax.fori_loop(0, out_ref.shape[1] // 8, one_group, 0, unroll=2)


def per_device(vels, skies, psi_maps, phi_maps, psf_taps, shifts):
    frames, share, width = psi_maps.shape
    maps = 2 * frames
    tiles = width // LANES
    rows = share * vels
    trials = shifts.shape[0]
    dma = pltpu.SemaphoreType.DMA
    blurred = pl.pallas_call(
        functools.partial(gather_kernel, vels, skies),
        out_shape=jax.ShapeDtypeStruct((maps, tiles + 1, rows + 2 * SHIFT, LANES), jnp.float32),
        in_specs=[
            pl.BlockSpec(memory_space=pltpu.SMEM),
            pl.BlockSpec(memory_space=pl.ANY),
            pl.BlockSpec(memory_space=pl.ANY),
        ],
        out_specs=pl.BlockSpec(memory_space=pltpu.VMEM),
        scratch_shapes=[
            pltpu.VMEM((vels, maps, share, width), jnp.float32),
            pltpu.VMEM((maps, tiles + 1, rows + 2 * EDGE, LANES), jnp.float32),
            pltpu.VMEM((maps, EDGE, width), jnp.float32),
            pltpu.VMEM((maps, EDGE, width), jnp.float32),
            pltpu.VMEM((2, 2, 2 * LANES, LANES), jnp.bfloat16),
            pltpu.VMEM((2, psf_taps.shape[0], 8, LANES), jnp.float32),
            dma((2,)),
            dma((vels, maps)),
            dma((vels // 2, maps)),
            dma((vels // 2, maps)),
            dma((vels // 2, maps)),
            dma((maps,)),
            dma((maps,)),
            dma((maps,)),
            dma((maps,)),
        ],
        compiler_params=pltpu.CompilerParams(
            collective_id=0, has_side_effects=True, vmem_limit_bytes=24 * 2**20
        ),
        name="gather",
    )(psf_taps, psi_maps, phi_maps)
    return pl.pallas_call(
        stack_kernel,
        grid=(trials,),
        out_shape=jax.ShapeDtypeStruct((trials, rows, width), jnp.float32),
        in_specs=[
            pl.BlockSpec(memory_space=pltpu.SMEM),
            pl.BlockSpec(memory_space=pltpu.VMEM),
        ],
        out_specs=pl.BlockSpec((1, rows, width), lambda t: (t, 0, 0)),
        compiler_params=pltpu.CompilerParams(vmem_limit_bytes=4 * 2**20),
        name="stack",
    )(shifts, blurred)


def solution(mesh):
    return jax.shard_map(
        functools.partial(per_device, mesh.shape["vel"], mesh.shape["sky"]),
        mesh=mesh,
        in_specs=(
            P(None, ("sky", "vel"), None),
            P(None, ("sky", "vel"), None),
            P(),
            P("vel", None, None),
        ),
        out_specs=P("vel", "sky", None),
        check_vma=False,
    )
```

time: 327 us -> 128 us (0.39); the launches traced: 323 us -> 127 us
  Pallas kernels: 0 us -> 124 us
  waiting for transfers between devices: 94.3 us -> 0 us
  loops' own time: 84 us -> 0 us
  other arithmetic: 58.2 us -> 0 us
  local copies, waits for them, and re-layouts: 47.8 us -> 3.52 us
  matrix products: 14 us -> 0 us
  between operations: 13.5 us -> 0.01 us
  starting transfers between devices: 11 us -> 0 us
    pallas_call x0 -> x2, Pallas kernels: none -> 124 us  [the longest x1 81.6 us: per_device(): pl.pallas_call(functools.partial(gather_kernel, vels, skies), out_shape=j...]
    another operation x1 -> x0, loops' own time: 84 us -> none  [per_device(): return lax.map(stack_trial, shifts)]
    all_gather x1 -> x0, waiting for transfers between devices: 83.7 us -> none  [per_device(): blurred = lax.all_gather(share_blur, 'vel', axis=2, tiled=True)]
    slice x18 -> x0, local copies, waits for them, and re-layouts: 47.7 us -> none  [the longest x8 40.5 us: stack_trial(): reach[:, frame]]
    add x9 -> x0, other arithmetic: 20.6 us -> none  [the longest x8 18.6 us: stack_trial(): total = total + piece]
    dot_general x2 -> x0, matrix products: 14 us -> none  [the longest x1 7 us: correlate(): jnp.matmul(extended[0], band_matrix(weights, width), precision=lax.Precis...]
    concatenate x2 -> x0, other arithmetic: 12.4 us -> none  [padded(): jnp.concatenate([lax.ppermute(tail, axis, [(i, (i + 1) % count) for i in...]
    another operation x9 -> x0, other arithmetic: 12 us -> none  [correlate(): factor = jnp.stack([weights[position], squared[position]])]
  transfers between devices with their start and end apart: 5 -> 0, of which waited for: 3 -> 0; matrix products, arithmetic and copies ran while one was open for 5% -> 0% of each run, Pallas kernels for 0% -> 0%
where the time goes in v1:
time: 128 us; the launch traced here: 127 us
  Pallas kernels  124 us (97%)
  local copies, waits for them, and re-layouts  3.52 us (3%)
    pallas_call x1, Pallas kernels, per_device(): pl.pallas_call(functools.partial(gather_kernel, vels, skies), out_shape=j...  81.6 us
    pallas_call x1, Pallas kernels, per_device(): pl.pallas_call(stack_kernel, grid=(trials,), out_shape=jax.ShapeDtypeStru...  42.3 us
    unnamed x7, local copies, waits for them, and re-layouts  3.52 us

profile of v1, /device:TPU:3, one launch (start us, length us, event | category | flops | bytes accessed | tf_op | source)
XLA Modules:
  0.0 127.5 jit_solution(1944508410310558841)
XLA Ops:
  0.0 0.8 copy.5.shifts_ref
  0.8 0.0 copy-start
  0.8 1.0 copy-done
  1.8 0.0 copy-start.1
  1.8 1.0 copy-done.1
  2.9 0.0 copy-start.2
  2.9 0.7 copy-done.2
  3.5 81.6 %gather.1.maps_ref = f32[8,5,544,128]{3,2,1,0:T(8,128)S(1)} custom-call(f32[9]{0:T(128)S(1)} %copy-done.2, f32[4,64,512]{2,1,0:T(8,128)S(1)} %copy-done, f32[4,64,512]{2,1,0:T(8,128)S(1)} %copy-done.1), custom_call_target="tpu_custom_call" | custom-call | tf_op jit(solution)/shard_map/gather/pallas_call | solution.py:353
  85.2 42.3 %stack.1 = f32[8,512,512]{2,1,0:T(8,128)} custom-call(s32[8,4,2]{2,1,0:T(4,128)S(1)} %copy.5.shifts_ref, f32[8,5,544,128]{3,2,1,0:T(8,128)S(1)} %gather.1.maps_ref), custom_call_target="tpu_custom_call" | custom-call | tf_op jit(solution)/shard_map/stack/pallas_call | solution.py:384
Async XLA Ops:
  0.8 1.0 copy-start
  1.8 1.0 copy-start.1
  2.9 0.7 copy-start.2

commit v2 on v1

--- a/solution.py
+++ b/solution.py
@@ -125,37 +125,48 @@
         value = jnp.full((8, LANES), taps_ref[i], jnp.float32) * scale
         weight[0, i] = value
         weight[1, i] = value * value
-    place = lax.broadcasted_iota(jnp.int32, (2 * LANES, LANES), 0)
-    place = place - lax.broadcasted_iota(jnp.int32, (2 * LANES, LANES), 1)
-    place = place - (LANES - SHIFT - half)
-    for kind in range(2):
-        matrix = jnp.zeros((2 * LANES, LANES), jnp.float32)
-        for i in range(taps):
-            value = jnp.broadcast_to(weight[kind, i][:1], (2 * LANES, LANES))
-            matrix = jnp.where(place == i, value, matrix)
-        coarse = matrix.astype(jnp.bfloat16)
-        band[kind, 0] = coarse
-        band[kind, 1] = (matrix - coarse.astype(jnp.float32)).astype(jnp.bfloat16)
+    place = lax.broadcasted_iota(jnp.int32, (3 * LANES, LANES), 0)
+    place = place - lax.broadcasted_iota(jnp.int32, (3 * LANES, LANES), 1)
+    for lead in range(2):
+        spot = place - (LANES - SHIFT * lead - half)
+        for kind in range(2):
+            matrix = jnp.zeros((3 * LANES, LANES), jnp.float32)
+            for i in range(taps):
+                value = jnp.broadcast_to(weight[kind, i][:1], (3 * LANES, LANES))
+                matrix = jnp.where(spot == i, value, matrix)
+            coarse = matrix.astype(jnp.bfloat16)
+            band[lead, kind, 0] = coarse
+            band[lead, kind, 1] = (matrix - coarse.astype(jnp.float32)).astype(jnp.bfloat16)
 
     def blur_along(block, m, start):
         kind = m // frames
         count = block.shape[0]
         coarse = block.astype(jnp.bfloat16)
         fine = (block - coarse.astype(jnp.float32)).astype(jnp.bfloat16)
-        for tile in range(tiles + 1):
-            first, last = max(tile - 1, 0), min(tile + 1, tiles)
-            columns = slice(first * LANES, last * LANES)
-            offset = (first - tile + 1) * LANES
-            depth = (last - first) * LANES
-            high = band[kind, 0, offset : offset + depth]
-            low = band[kind, 1, offset : offset + depth]
-            value = jnp.dot(coarse[:, columns], high, preferred_element_type=jnp.float32)
-            value += jnp.dot(fine[:, columns], high, preferred_element_type=jnp.float32)
-            value += jnp.dot(coarse[:, columns], low, preferred_element_type=jnp.float32)
-            if tile in (0, tiles):
-                lane = lax.broadcasted_iota(jnp.int32, (count, LANES), 1)
-                value = jnp.where(lane >= SHIFT if tile == 0 else lane < SHIFT, value, 0.0)
-            along[m, tile, pl.ds(start, count)] = value
+
+        def place_tiles(lead):
+            for tile in range(tiles + lead):
+                first, last = max(tile - 1, 0), min(tile + 2 - lead, tiles)
+                columns = slice(first * LANES, last * LANES)
+                offset = (first - tile + 1) * LANES
+                depth = (last - first) * LANES
+                high = band[lead, kind, 0, offset : offset + depth]
+                low = band[lead, kind, 1, offset : offset + depth]
+                value = jnp.dot(coarse[:, columns], high, preferred_element_type=jnp.float32)
+                value += jnp.dot(fine[:, columns], high, preferred_element_type=jnp.float32)
+                value += jnp.dot(coarse[:, columns], low, preferred_element_type=jnp.float32)
+                if lead and tile in (0, tiles):
+                    lane = lax.broadcasted_iota(jnp.int32, (count, LANES), 1)
+                    value = jnp.where(lane >= SHIFT if tile == 0 else lane < SHIFT, value, 0.0)
+                along[m, tile, pl.ds(start, count)] = value
+
+        @pl.when(m % frames == 0)
+        def _():
+            place_tiles(0)
+
+        @pl.when(m % frames > 0)
+        def _():
+            place_tiles(1)
 
     def blur_across(m, start, count):
         kind = m // frames
@@ -170,7 +181,7 @@
                 out_ref[m, tile, pl.ds(pl.multiple_of(base, 8), 8)] = value
             return carry
 
-        lax.fori_loop(0, tiles + 1, one_tile, 0)
+        lax.fori_loop(0, tiles + jnp.minimum(m % frames, 1), one_tile, 0)
 
     def arrive(distance, m):
         left = chip - distance
@@ -310,26 +321,26 @@
     trial = pl.program_id(0)
     lane = lax.broadcasted_iota(jnp.int32, (8, LANES), 1)
     down, turn, inside = [], [], []
-    for frame in range(frames):
+    for frame in range(1, frames):
         offset = shifts_ref[trial, frame, 1] + SHIFT
         down.append(shifts_ref[trial, frame, 0] + SHIFT)
         turn.append(lax.rem(LANES - offset, LANES))
-        inside.append(lane < LANES - offset)
+        inside.append(lane >= offset)
 
     def one_group(group, carry):
         base = group * 8
 
         def stacked(kind):
-            total = [None] * (tiles - 1)
-            for frame in range(frames):
-                m = kind * frames + frame
-                rolled = [
-                    pltpu.roll(maps_ref[m, tile, pl.ds(base + down[frame], 8)], turn[frame], 1)
-                    for tile in range(tiles)
-                ]
+            total = [
+                maps_ref[kind * frames, tile, pl.ds(pl.multiple_of(base + SHIFT, 8), 8)]
+                for tile in range(tiles - 1)
+            ]
+            for step in range(frames - 1):
+                m = kind * frames + step + 1
+                pieces = [maps_ref[m, tile, pl.ds(base + down[step], 8)] for tile in range(tiles)]
                 for tile in range(tiles - 1):
-                    piece = jnp.where(inside[frame], rolled[tile], rolled[tile + 1])
-                    total[tile] = piece if frame == 0 else total[tile] + piece
+                    joined = jnp.where(inside[step], pieces[tile], pieces[tile + 1])
+                    total[tile] = total[tile] + pltpu.roll(joined, turn[step], 1)
             return total
 
         psi = stacked(0)
@@ -340,7 +351,7 @@
             )
         return carry
 
-    lax.fori_loop(0, out_ref.shape[1] // 8, one_group, 0, unroll=2)
+    lax.fori_loop(0, out_ref.shape[1] // 8, one_group, 0, unroll=8)
 
 
 def per_device(vels, skies, psi_maps, phi_maps, psf_taps, shifts):
@@ -364,7 +375,7 @@
             pltpu.VMEM((maps, tiles + 1, rows + 2 * EDGE, LANES), jnp.float32),
             pltpu.VMEM((maps, EDGE, width), jnp.float32),
             pltpu.VMEM((maps, EDGE, width), jnp.float32),
-            pltpu.VMEM((2, 2, 2 * LANES, LANES), jnp.bfloat16),
+            pltpu.VMEM((2, 2, 2, 3 * LANES, LANES), jnp.bfloat16),
             pltpu.VMEM((2, psf_taps.shape[0], 8, LANES), jnp.float32),
             dma((2,)),
             dma((vels, maps)),

time: 128 us -> 106 us (0.83)
  Pallas kernels: 124 us -> 102 us
    pallas_call x1, Pallas kernels: 42.3 us -> 20.2 us  [per_device(): pl.pallas_call(stack_kernel, grid=(trials,), out_shape=jax.ShapeDtypeStru...]
where the time goes in v2:
time: 106 us
  Pallas kernels  102 us (96%)
  local copies, waits for them, and re-layouts  3.52 us (3%)
    pallas_call x1, Pallas kernels, per_device(): pl.pallas_call(functools.partial(gather_kernel, vels, skies), out_shape=j...  81.8 us
    pallas_call x1, Pallas kernels, per_device(): pl.pallas_call(stack_kernel, grid=(trials,), out_shape=jax.ShapeDtypeStru...  20.2 us
    unnamed x7, local copies, waits for them, and re-layouts  3.52 us

profile of v2, /device:TPU:3, one launch (start us, length us, event | category | flops | bytes accessed | tf_op | source)
XLA Modules:
  0.0 105.6 jit_solution(5908775272937601539)
XLA Ops:
  0.0 0.8 copy.5.shifts_ref
  0.8 0.0 copy-start
  0.8 1.0 copy-done
  1.8 0.0 copy-start.1
  1.8 1.0 copy-done.1
  2.9 0.0 copy-start.2
  2.9 0.7 copy-done.2
  3.5 81.8 %gather.1.maps_ref = f32[8,5,544,128]{3,2,1,0:T(8,128)S(1)} custom-call(f32[9]{0:T(128)S(1)} %copy-done.2, f32[4,64,512]{2,1,0:T(8,128)S(1)} %copy-done, f32[4,64,512]{2,1,0:T(8,128)S(1)} %copy-done.1), custom_call_target="tpu_custom_call" | custom-call | tf_op jit(solution)/shard_map/gather/pallas_call | solution.py:364
  85.4 20.2 %stack.1 = f32[8,512,512]{2,1,0:T(8,128)} custom-call(s32[8,4,2]{2,1,0:T(4,128)S(1)} %copy.5.shifts_ref, f32[8,5,544,128]{3,2,1,0:T(8,128)S(1)} %gather.1.maps_ref), custom_call_target="tpu_custom_call" | custom-call | tf_op jit(solution)/shard_map/stack/pallas_call | solution.py:395
Async XLA Ops:
  0.8 1.0 copy-start
  1.8 1.0 copy-start.1
  2.9 0.7 copy-start.2

commit v3 on v2

--- a/solution.py
+++ b/solution.py
@@ -12,8 +12,94 @@
 MESH = pl.DeviceIdType.MESH
 
 
+def stack_rows(shifts_ref, maps_ref, out_ref, trial, first, count, shift, unroll):
+    frames = shifts_ref.shape[1]
+    tiles = maps_ref.shape[1]
+    lane = lax.broadcasted_iota(jnp.int32, (8, LANES), 1)
+    down, turn, inside = [], [], []
+    for frame in range(1, frames):
+        offset = shifts_ref[trial, frame, 1] + SHIFT
+        down.append(shifts_ref[trial, frame, 0] + SHIFT)
+        turn.append(lax.rem(LANES - offset, LANES))
+        inside.append(lane >= offset)
+
+    def one_group(group, carry):
+        base = first + group * 8
+
+        def stacked(kind):
+            total = [
+                maps_ref[kind * frames, tile, pl.ds(pl.multiple_of(base + SHIFT, 8), 8)]
+                for tile in range(tiles - 1)
+            ]
+            for step in range(frames - 1):
+                m = kind * frames + step + 1
+                pieces = [maps_ref[m, tile, pl.ds(base + down[step], 8)] for tile in range(tiles)]
+                for tile in range(tiles - 1):
+                    joined = jnp.where(inside[step], pieces[tile], pieces[tile + 1])
+                    total[tile] = total[tile] + pltpu.roll(joined, turn[step], 1)
+            return total
+
+        psi = stacked(0)
+        phi = stacked(1)
+        for tile in range(tiles - 1):
+            out_ref[
+                trial, pl.ds(pl.multiple_of(base - shift, 8), 8), tile * LANES : (tile + 1) * LANES
+            ] = psi[tile] * lax.rsqrt(phi[tile])
+        return carry
+
+    lax.fori_loop(0, count // 8, one_group, 0, unroll=unroll)
+
+
+def stack_kernel(vels, shifts_ref, maps_ref, done_ref, out_ref, near, far, sems):
+    trials, rows, _ = done_ref.shape
+    both = 2 * (rows // vels)
+    chip = lax.axis_index("vel") // 2
+    low = (chip < vels // 4).astype(jnp.int32)
+    middle = rows - both - 2 * EDGE
+    middle_row = pl.multiple_of(EDGE + (1 - low) * both, 8)
+    near_row = pl.multiple_of((1 - low) * (rows - EDGE), 8)
+    far_row = pl.multiple_of(low * (rows - both - EDGE), 8)
+
+    def middle_copy(trial):
+        part = pl.ds(middle_row, middle)
+        return pltpu.make_async_copy(done_ref.at[trial, part], out_ref.at[trial, part], sems.at[0, trial])
+
+    def near_copy(trial):
+        return pltpu.make_async_copy(
+            near.at[trial], out_ref.at[trial, pl.ds(near_row, EDGE)], sems.at[1, trial]
+        )
+
+    def far_copy(trial):
+        return pltpu.make_async_copy(
+            far.at[trial], out_ref.at[trial, pl.ds(far_row, both + EDGE)], sems.at[2, trial]
+        )
+
+    def begin(trial, carry):
+        middle_copy(trial).start()
+        return carry
+
+    lax.fori_loop(0, trials, begin, 0)
+
+    def compute(trial, carry):
+        stack_rows(shifts_ref, maps_ref, near, trial, near_row, EDGE, near_row, 3)
+        near_copy(trial).start()
+        stack_rows(shifts_ref, maps_ref, far, trial, far_row, both + EDGE, far_row, True)
+        far_copy(trial).start()
+        return carry
+
+    lax.fori_loop(0, trials, compute, 0)
+
+    def finish(trial, carry):
+        middle_copy(trial).wait()
+        near_copy(trial).wait()
+        far_copy(trial).wait()
+        return carry
+
+    lax.fori_loop(0, trials, finish, 0)
+
+
 def gather_kernel(
-    vels, skies, taps_ref, psi_ref, phi_ref, out_ref,
+    vels, skies, taps_ref, shifts_ref, psi_ref, phi_ref, out_ref, done_ref,
     raw, along, top, bottom, band, weight,
     own_sem, recv_sem, right_sem, left_sem, pair_sem, top_recv, bottom_recv, top_send, bottom_send,
 ):
@@ -242,6 +328,27 @@
 
         lax.fori_loop(0, 2, one_side, 0)
 
+    lead = jnp.where(chip < chips // 2, chips - 1, 0)
+
+    def stack_side(distance, trial):
+        def one_side(side, carry):
+            origin = chip + (2 * side - 1) * distance
+            wanted = (origin >= 0) & (origin < chips) & (origin != lead)
+
+            @pl.when(wanted & (distance == 0) & (side == 0))
+            def _():
+                first = origin * both + EDGE
+                stack_rows(shifts_ref, out_ref, done_ref, trial, first, both - 2 * EDGE, 0, 2)
+
+            @pl.when(wanted & (distance > 0))
+            def _():
+                first = origin * both + EDGE - 2 * EDGE * side
+                stack_rows(shifts_ref, out_ref, done_ref, trial, first, both, 0, 8)
+
+            return carry
+
+        lax.fori_loop(0, 2, one_side, 0)
+
     def step(index, carry):
         @pl.when(index < chips * maps)
         def _():
@@ -250,6 +357,15 @@
         @pl.when(index > 0)
         def _():
             process((index - 1) // maps, (index - 1) % maps)
+
+        @pl.when(index > maps)
+        def _():
+            for block in range(0, shifts_ref.shape[0], maps):
+                trial = (index - 1) % maps + block
+
+                @pl.when(trial < shifts_ref.shape[0])
+                def _(trial=trial):
+                    stack_side((index - 1) // maps - 1, trial)
 
         return carry
 
@@ -313,45 +429,6 @@
         return carry
 
     lax.fori_loop(0, chips * maps, drain, 0)
-
-
-def stack_kernel(shifts_ref, maps_ref, out_ref):
-    frames = shifts_ref.shape[1]
-    tiles = maps_ref.shape[1]
-    trial = pl.program_id(0)
-    lane = lax.broadcasted_iota(jnp.int32, (8, LANES), 1)
-    down, turn, inside = [], [], []
-    for frame in range(1, frames):
-        offset = shifts_ref[trial, frame, 1] + SHIFT
-        down.append(shifts_ref[trial, frame, 0] + SHIFT)
-        turn.append(lax.rem(LANES - offset, LANES))
-        inside.append(lane >= offset)
-
-    def one_group(group, carry):
-        base = group * 8
-
-        def stacked(kind):
-            total = [
-                maps_ref[kind * frames, tile, pl.ds(pl.multiple_of(base + SHIFT, 8), 8)]
-                for tile in range(tiles - 1)
-            ]
-            for step in range(frames - 1):
-                m = kind * frames + step + 1
-                pieces = [maps_ref[m, tile, pl.ds(base + down[step], 8)] for tile in range(tiles)]
-                for tile in range(tiles - 1):
-                    joined = jnp.where(inside[step], pieces[tile], pieces[tile + 1])
-                    total[tile] = total[tile] + pltpu.roll(joined, turn[step], 1)
-            return total
-
-        psi = stacked(0)
-        phi = stacked(1)
-        for tile in range(tiles - 1):
-            out_ref[0, pl.ds(pl.multiple_of(base, 8), 8), tile * LANES : (tile + 1) * LANES] = (
-                psi[tile] * lax.rsqrt(phi[tile])
-            )
-        return carry
-
-    lax.fori_loop(0, out_ref.shape[1] // 8, one_group, 0, unroll=8)
 
 
 def per_device(vels, skies, psi_maps, phi_maps, psf_taps, shifts):
@@ -361,15 +438,19 @@
     rows = share * vels
     trials = shifts.shape[0]
     dma = pltpu.SemaphoreType.DMA
-    blurred = pl.pallas_call(
+    blurred, done = pl.pallas_call(
         functools.partial(gather_kernel, vels, skies),
-        out_shape=jax.ShapeDtypeStruct((maps, tiles + 1, rows + 2 * SHIFT, LANES), jnp.float32),
+        out_shape=(
+            jax.ShapeDtypeStruct((maps, tiles + 1, rows + 2 * SHIFT, LANES), jnp.float32),
+            jax.ShapeDtypeStruct((trials, rows, width), jnp.float32),
+        ),
         in_specs=[
+            pl.BlockSpec(memory_space=pltpu.SMEM),
             pl.BlockSpec(memory_space=pltpu.SMEM),
             pl.BlockSpec(memory_space=pl.ANY),
             pl.BlockSpec(memory_space=pl.ANY),
         ],
-        out_specs=pl.BlockSpec(memory_space=pltpu.VMEM),
+        out_specs=(pl.BlockSpec(memory_space=pltpu.VMEM), pl.BlockSpec(memory_space=pltpu.VMEM)),
         scratch_shapes=[
             pltpu.VMEM((vels, maps, share, width), jnp.float32),
             pltpu.VMEM((maps, tiles + 1, rows + 2 * EDGE, LANES), jnp.float32),
@@ -391,19 +472,24 @@
             collective_id=0, has_side_effects=True, vmem_limit_bytes=24 * 2**20
         ),
         name="gather",
-    )(psf_taps, psi_maps, phi_maps)
+    )(psf_taps, shifts, psi_maps, phi_maps)
     return pl.pallas_call(
-        stack_kernel,
-        grid=(trials,),
+        functools.partial(stack_kernel, vels),
         out_shape=jax.ShapeDtypeStruct((trials, rows, width), jnp.float32),
         in_specs=[
             pl.BlockSpec(memory_space=pltpu.SMEM),
             pl.BlockSpec(memory_space=pltpu.VMEM),
+            pl.BlockSpec(memory_space=pltpu.VMEM),
         ],
-        out_specs=pl.BlockSpec((1, rows, width), lambda t: (t, 0, 0)),
+        out_specs=pl.BlockSpec(memory_space=pl.ANY),
+        scratch_shapes=[
+            pltpu.VMEM((trials, EDGE, width), jnp.float32),
+            pltpu.VMEM((trials, 2 * share + EDGE, width), jnp.float32),
+            dma((3, trials)),
+        ],
         compiler_params=pltpu.CompilerParams(vmem_limit_bytes=4 * 2**20),
         name="stack",
-    )(shifts, blurred)
+    )(shifts, blurred, done)
 
 
 def solution(mesh):

time: 106 us -> 93.8 us (0.88)
  Pallas kernels: 102 us -> 90.1 us
    pallas_call x2, Pallas kernels: 102 us -> 90.1 us  [the longest x1 82.9 us: per_device(): pl.pallas_call(functools.partial(gather_kernel, vels, skies), out_shape=(...]
where the time goes in v3:
time: 93.8 us; the launch traced here: 93.6 us
  Pallas kernels  90.1 us (96%)
  local copies, waits for them, and re-layouts  3.52 us (4%)
    pallas_call x1, Pallas kernels, per_device(): pl.pallas_call(functools.partial(gather_kernel, vels, skies), out_shape=(...  82.9 us
    pallas_call x1, Pallas kernels, per_device(): pl.pallas_call(functools.partial(stack_kernel, vels), out_shape=jax.Shape...  7.13 us
    unnamed x7, local copies, waits for them, and re-layouts  3.52 us

profile of v3, /device:TPU:3, one launch (start us, length us, event | category | flops | bytes accessed | tf_op | source)
XLA Modules:
  0.0 93.6 jit_solution(2788870254914173486)
XLA Ops:
  0.0 0.8 copy.6.shifts_ref
  0.8 0.0 copy-start
  0.8 1.0 %copy-done = f32[4,64,512]{2,1,0:T(8,128)S(1)} copy-done((f32[4,64,512]{2,1,0:T(8,128)S(1)}, f32[4,64,512]{2,1,0:T(8,128)}, u32[]{:S(2)}) %copy-start) | copy-done | bytes 524312
  1.8 0.0 copy-start.1
  1.8 1.0 %copy-done.1 = f32[4,64,512]{2,1,0:T(8,128)S(1)} copy-done((f32[4,64,512]{2,1,0:T(8,128)S(1)}, f32[4,64,512]{2,1,0:T(8,128)}, u32[]{:S(2)}) %copy-start.1) | copy-done | bytes 524312
  2.9 0.0 copy-start.2
  2.9 0.7 copy-done.2
  3.5 82.9 %gather.1 = (f32[8,5,544,128]{3,2,1,0:T(8,128)S(1)}, f32[8,512,512]{2,1,0:T(8,128)S(1)}) custom-call(f32[9]{0:T(128)S(1)} %copy-done.2, s32[8,4,2]{2,1,0:T(4,128)S(1)} %copy.6.shifts_ref, f32[4,64,512]{2,1,0:T(8,128)S(1)} %copy-done, f32[4,64,512]{2,1,0:T(8,128)S(1)} %copy-done.1), custom_call_target="tpu_custom_call" | custom-call | tf_op jit(solution)/shard_map/gather/pallas_call | solution.py:441
  86.5 7.1 %stack.1 = f32[8,512,512]{2,1,0:T(8,128)} custom-call(s32[8,4,2]{2,1,0:T(4,128)S(1)} %copy.6.shifts_ref, f32[8,5,544,128]{3,2,1,0:T(8,128)S(1)} %get-tuple-element.7.maps_ref, f32[8,512,512]{2,1,0:T(8,128)S(1)} %get-tuple-element.8.done_ref), custom_call_target="tpu_custom_call" | custom-call | tf_op jit(solution)/shard_map/stack/pallas_call | solution.py:476
Async XLA Ops:
  0.8 1.0 %copy-start = (f32[4,64,512]{2,1,0:T(8,128)S(1)}, f32[4,64,512]{2,1,0:T(8,128)}, u32[]{:S(2)}) copy-start(f32[4,64,512]{2,1,0:T(8,128)} %psi_ref.1) | copy-start | bytes 1572868
  1.8 1.0 %copy-start.1 = (f32[4,64,512]{2,1,0:T(8,128)S(1)}, f32[4,64,512]{2,1,0:T(8,128)}, u32[]{:S(2)}) copy-start(f32[4,64,512]{2,1,0:T(8,128)} %phi_ref.1) | copy-start | bytes 1572868
  2.9 0.7 copy-start.2

commit v4 on v3

--- a/solution.py
+++ b/solution.py
@@ -144,9 +144,6 @@
     for present, _ in neighbours:
         peers = peers + present.astype(jnp.int32)
     pl.semaphore_wait(barrier, peers)
-    own_psi.wait()
-    own_phi.wait()
-
     def line_copy(origin, m, to_right):
         chunk = 2 * origin + core
         return pltpu.make_async_remote_copy(
@@ -201,7 +198,10 @@
         pair_copy(chip, m, core).start()
         return carry
 
-    lax.fori_loop(0, maps, send_own, 0)
+    own_psi.wait()
+    lax.fori_loop(0, frames, send_own, 0)
+    own_phi.wait()
+    lax.fori_loop(frames, maps, send_own, 0)
 
     total = taps_ref[0]
     for i in range(1, taps):

time: 93.8 us -> 93.8 us (level)
  no operation moved by 1% of the time
where the time goes in v4:
time: 93.8 us; the launch traced here: 93.6 us
  Pallas kernels  90.1 us (96%)
  local copies, waits for them, and re-layouts  3.52 us (4%)
    pallas_call x1, Pallas kernels, per_device(): pl.pallas_call(functools.partial(gather_kernel, vels, skies), out_shape=(...  82.9 us
    pallas_call x1, Pallas kernels, per_device(): pl.pallas_call(functools.partial(stack_kernel, vels), out_shape=jax.Shape...  7.14 us
    unnamed x7, local copies, waits for them, and re-layouts  3.52 us

profile of v4, /device:TPU:3, one launch (start us, length us, event | category | flops | bytes accessed | tf_op | source)
XLA Modules:
  0.0 93.6 jit_solution(18301718099015497225)
XLA Ops:
  0.0 0.8 copy.6.shifts_ref
  0.8 0.0 copy-start
  0.8 1.0 %copy-done = f32[4,64,512]{2,1,0:T(8,128)S(1)} copy-done((f32[4,64,512]{2,1,0:T(8,128)S(1)}, f32[4,64,512]{2,1,0:T(8,128)}, u32[]{:S(2)}) %copy-start) | copy-done | bytes 524312
  1.8 0.0 copy-start.1
  1.8 1.0 %copy-done.1 = f32[4,64,512]{2,1,0:T(8,128)S(1)} copy-done((f32[4,64,512]{2,1,0:T(8,128)S(1)}, f32[4,64,512]{2,1,0:T(8,128)}, u32[]{:S(2)}) %copy-start.1) | copy-done | bytes 524312
  2.9 0.0 copy-start.2
  2.9 0.7 copy-done.2
  3.5 82.9 %gather.1 = (f32[8,5,544,128]{3,2,1,0:T(8,128)S(1)}, f32[8,512,512]{2,1,0:T(8,128)S(1)}) custom-call(f32[9]{0:T(128)S(1)} %copy-done.2, s32[8,4,2]{2,1,0:T(4,128)S(1)} %copy.6.shifts_ref, f32[4,64,512]{2,1,0:T(8,128)S(1)} %copy-done, f32[4,64,512]{2,1,0:T(8,128)S(1)} %copy-done.1), custom_call_target="tpu_custom_call" | custom-call | tf_op jit(solution)/shard_map/gather/pallas_call | solution.py:441
  86.5 7.1 %stack.1 = f32[8,512,512]{2,1,0:T(8,128)} custom-call(s32[8,4,2]{2,1,0:T(4,128)S(1)} %copy.6.shifts_ref, f32[8,5,544,128]{3,2,1,0:T(8,128)S(1)} %get-tuple-element.7.maps_ref, f32[8,512,512]{2,1,0:T(8,128)S(1)} %get-tuple-element.8.done_ref), custom_call_target="tpu_custom_call" | custom-call | tf_op jit(solution)/shard_map/stack/pallas_call | solution.py:476
Async XLA Ops:
  0.8 1.0 %copy-start = (f32[4,64,512]{2,1,0:T(8,128)S(1)}, f32[4,64,512]{2,1,0:T(8,128)}, u32[]{:S(2)}) copy-start(f32[4,64,512]{2,1,0:T(8,128)} %psi_ref.1) | copy-start | bytes 1572868
  1.8 1.0 %copy-start.1 = (f32[4,64,512]{2,1,0:T(8,128)S(1)}, f32[4,64,512]{2,1,0:T(8,128)}, u32[]{:S(2)}) copy-start(f32[4,64,512]{2,1,0:T(8,128)} %phi_ref.1) | copy-start | bytes 1572868
  2.9 0.7 copy-start.2
